TPU v7x, 512 devices: a whole 4x8x8 slice. The times are simulated.
512 devices in a mesh: region: 32 (over x, z), batch: 16 (over y, core).
Axes of the slice: x: 4, y: 8, z: 8, core: 2. Of those that a mesh axis runs over, the one named last changes fastest.
Arguments:
- basis_values: bfloat16 [128, 2, 4096, 512], P('region', None, 'batch'), may hold values from -6 to 6
- dens_tiles: bfloat16 [128, 512, 512], P('region', 'batch'), may hold values from -0.005859375 to 0.005859375
- region_tiles: int32 [128, 3], replicated, may hold values from 0 to 127, as said below
- point_counts: int32 [128, 16], P('region', 'batch'), may hold values from 64 to 256, as said below
- point_weights: float32 [128, 4096], P('region', 'batch'), may hold values from 0.0078125 to 0.03125
Outputs:
- xc_tiles: float32 [128, 512, 512], P('region', 'batch')
Inputs may be any that keep to these rules, and one draw needn't show every extreme that they name: `region_tiles`: tile t is stored on index t // 4 of region. Regions 4 * i to 4 * i + 3 lie on index i; among their 12 entries no owner index holds more than 1 and some owner holds exactly 1, on every index; the entries of one owner on one index are different tiles. `point_counts`: every region has at least one batch with all 256 points live.
All inputs are finite; a program needn't handle non-finite values.
Results may differ from a plain program's by a relative error of at most 0.004.
Values may be sent and summed in bfloat16 or wider, within the bound.
A program may use at most 64 MiB of HBM per device.

v0:
```python
import jax
import jax.numpy as jnp
from jax import lax
from jax.sharding import PartitionSpec as P

SLATER = 0.9847450218426964


def potential(density):
    return -SLATER * density * jnp.power(density * density + 1.0, -1.0 / 3.0)


def shards(basis_values, dens_tiles, region_tiles, point_counts, point_weights):
    owner_count = lax.axis_size("region")
    batch_count = lax.axis_size("batch")
    my_index = lax.axis_index("region")
    region_local = basis_values.shape[0]
    point_local = basis_values.shape[2]
    tile_local = dens_tiles.shape[0]
    row_count = dens_tiles.shape[1]
    block_width = dens_tiles.shape[2]
    requests = 3 * region_local
    slot_total = (requests + owner_count - 1) // owner_count
    table = region_tiles.reshape(owner_count, requests)
    owners = table // tile_local
    local_ids = table % tile_local
    order = jnp.arange(requests, dtype=jnp.int32)
    earlier = (owners[:, :, None] == owners[:, None, :]) & (
        order[None, None, :] < order[None, :, None]
    )
    ranks = jnp.sum(earlier.astype(jnp.int32), axis=2)
    slot_ids = jnp.arange(slot_total, dtype=jnp.int32)
    tile_ids = jnp.arange(tile_local, dtype=jnp.int32)
    chosen = (
        (owners == my_index)[:, :, None, None]
        & (ranks[:, :, None, None] == slot_ids[None, None, :, None])
        & (local_ids[:, :, None, None] == tile_ids[None, None, None, :])
    )
    selector = jnp.sum(chosen.astype(jnp.float32), axis=1)
    my_owners = lax.dynamic_index_in_dim(owners, my_index, 0, keepdims=False)
    my_ranks = lax.dynamic_index_in_dim(ranks, my_index, 0, keepdims=False)
    outgoing = jnp.einsum(
        "dct,trb->dcrb",
        selector.astype(jnp.bfloat16),
        dens_tiles,
        preferred_element_type=jnp.float32,
    ).astype(jnp.bfloat16)
    incoming = lax.all_to_all(outgoing, "region", split_axis=0, concat_axis=0, tiled=True)
    flat = incoming.reshape(owner_count * slot_total, row_count, block_width)
    fetched = jnp.take(flat, my_owners * slot_total + my_ranks, axis=0)
    piece = lax.all_gather(fetched, "batch", axis=1, tiled=True)
    count = piece.shape[1]
    shaped = piece.reshape(region_local, 3, count, block_width)
    left_aa = jnp.einsum(
        "rpc,rcb->rpb", basis_values[:, 0], shaped[:, 0], preferred_element_type=jnp.float32
    )
    left_ab = jnp.einsum(
        "rpc,rcb->rpb", basis_values[:, 0], shaped[:, 1], preferred_element_type=jnp.float32
    )
    left_bb = jnp.einsum(
        "rpc,rcb->rpb", basis_values[:, 1], shaped[:, 2], preferred_element_type=jnp.float32
    )
    left_aa, left_ab, left_bb = (left_aa, left_ab, left_bb)
    phi_a = basis_values[:, 0]
    phi_b = basis_values[:, 1]
    density = (
        jnp.sum(phi_a * left_aa, axis=-1)
        + 2.0 * jnp.sum(phi_b * left_ab, axis=-1)
        + jnp.sum(phi_b * left_bb, axis=-1)
    )
    live = jnp.arange(point_local, dtype=jnp.int32)[None, :] < point_counts
    scale = jnp.where(live, point_weights * potential(density), 0.0)
    scaled_a = (scale[:, :, None] * phi_a).astype(jnp.bfloat16)
    scaled_b = (scale[:, :, None] * phi_b).astype(jnp.bfloat16)
    first = jnp.einsum("rpc,rpb->crb", phi_a, scaled_a, preferred_element_type=jnp.float32)
    second = jnp.einsum("rpc,rpb->crb", phi_a, scaled_b, preferred_element_type=jnp.float32)
    third = jnp.einsum("rpc,rpb->crb", phi_b, scaled_b, preferred_element_type=jnp.float32)
    partial_pairs = jnp.stack([first, second, third], axis=2).reshape(
        block_width, requests, block_width
    )
    partial_pairs = partial_pairs.astype(jnp.bfloat16).reshape(
        batch_count, row_count, requests, block_width
    )
    received = lax.all_to_all(partial_pairs, "batch", split_axis=0, concat_axis=0, tiled=True)
    pairs = jnp.sum(received.astype(jnp.float32), axis=0)
    placement = (
        (my_owners[:, None, None] == jnp.arange(owner_count, dtype=jnp.int32)[None, :, None])
        & (my_ranks[:, None, None] == slot_ids[None, None, :])
    ).astype(jnp.float32)
    outgoing_sums = jnp.einsum("jdc,rjb->dcrb", placement, pairs, precision=lax.Precision.HIGHEST)
    returned = lax.all_to_all(outgoing_sums, "region", split_axis=0, concat_axis=0, tiled=True)
    return jnp.einsum("dct,dcrb->trb", selector, returned, precision=lax.Precision.HIGHEST)


def solution(mesh):
    return jax.shard_map(
        shards,
        mesh=mesh,
        in_specs=(
            P("region", None, "batch", None),
            P("region", "batch", None),
            P(),
            P("region", "batch"),
            P("region", "batch"),
        ),
        out_specs=P("region", "batch", None),
        check_vma=False,
    )
```

profile of v0, /device:TPU:1, one launch (start us, length us, event | category | flops | bytes accessed | tf_op | source)
XLA Modules:
  0.0 331.1 jit_solution(2894611914320594194)
XLA Ops:
  6.5 0.8 copy.81
  7.7 0.5 fusion.14
  8.2 1.6 copy.88
  9.8 13.8 %all-to-all-start = ((bf16[32,1,32,512]{3,2,1,0:T(8,128)(2,1)}), bf16[32,1,32,512]{3,2,1,0:T(8,128)(2,1)S(1)}, u32[]{:S(2)}, u32[]{:S(2)}) async-start(bf16[32,1,32,512]{3,2,1,0:T(8,128)(2,1)} %copy.88), calls=%async_computation | async-start | bytes 2097152 | tf_op jit(solution)/shard_map/all_to_all | solution.py:48
  24.0 24.3 %all-to-all-done = bf16[32,1,32,512]{3,2,1,0:T(8,128)(2,1)S(1)} async-done(((bf16[32,1,32,512]{3,2,1,0:T(8,128)(2,1)}), bf16[32,1,32,512]{3,2,1,0:T(8,128)(2,1)S(1)}, u32[]{:S(2)}, u32[]{:S(2)}) %all-to-all-start) | async-done | bytes 1048608 | tf_op jit(solution)/shard_map/all_to_all | solution.py:48
  48.3 1.4 gather_fusion
  49.6 1.9 broadcast_select_fusion
  51.5 49.9 %all-gather.2.cloned.1.call-done = bf16[12,512,512]{2,1,0:T(8,128)(2,1)} async-done(((bf16[12,32,512]{2,1,0:T(8,128)(2,1)}), bf16[12,512,512]{2,1,0:T(8,128)(2,1)}) %all-gather.2.cloned.1.call-update) | async-done | bytes 6291472 | tf_op jit(solution)/shard_map/all_gather | solution.py:51
  101.5 2.5 fusion.2
  104.0 0.9 copy-done.4
  104.9 0.8 fusion
  105.7 0.8 fusion.3
  106.6 0.9 convert_bitcast_fusion.1
  107.5 0.9 convert_bitcast_fusion
  108.4 0.9 convert_bitcast_fusion.2
  109.4 0.8 pad_maximum_fusion
  110.6 1.1 copy.100
  111.8 145.4 %all_to_all.15 = bf16[16,32,12,512]{3,1,2,0:T(8,128)(2,1)S(1)} all-to-all(bf16[16,32,12,512]{3,1,2,0:T(8,128)(2,1)S(1)} %copy.100), channel_id=1, replica_groups=mesh['region'=32,'batch'=16] {'batch'}, dimensions={0} | all-to-all | bytes 12582912 | tf_op jit(solution)/shard_map/all_to_all | solution.py:84
  257.1 1.3 convert_reduce_fusion
  258.4 1.4 convolution_bitcast_fusion
  259.8 1.2 copy.103
  261.0 60.3 %all_to_all.16 = f32[32,1,32,512]{3,2,1,0:T(8,128)S(1)} all-to-all(f32[32,1,32,512]{3,2,1,0:T(8,128)S(1)} %copy.103), channel_id=1, replica_groups=mesh['region'=32,'batch'=16] {'region'}, dimensions={0} | all-to-all | bytes 4194304 | tf_op jit(solution)/shard_map/all_to_all | solution.py:91
  321.3 2.2 fusion.8
  323.5 0.8 copy.105
  (24 shorter events, 1.1 us)
Async XLA Ops:
  6.5 1.2 copy-start
  9.8 91.7 %copy-start.1 = (bf16[4,2,256,512]{3,2,1,0:T(8,128)(2,1)S(1)}, bf16[4,2,256,512]{3,2,1,0:T(8,128)(2,1)}, u32[]{:S(2)}) copy-start(bf16[4,2,256,512]{3,2,1,0:T(8,128)(2,1)} %param.5) | copy-start | bytes 6291460
  9.8 38.5 %all-to-all-start = ((bf16[32,1,32,512]{3,2,1,0:T(8,128)(2,1)}), bf16[32,1,32,512]{3,2,1,0:T(8,128)(2,1)S(1)}, u32[]{:S(2)}, u32[]{:S(2)}) async-start(bf16[32,1,32,512]{3,2,1,0:T(8,128)(2,1)} %copy.88), calls=%async_computation | async-start | bytes 2097152 | tf_op jit(solution)/shard_map/all_to_all | solution.py:48
  23.6 77.8 %all-gather.2.cloned.1.call-start = ((), (), s32[]{:S(2)}) async-start(), calls=%async_computation.3 | async-start | bytes 6684672 | tf_op jit(solution)/shard_map/all_gather | solution.py:51
  101.5 3.4 %copy-start.4 = (bf16[12,512,512]{2,1,0:T(8,128)(2,1)S(1)}, bf16[12,512,512]{2,1,0:T(8,128)(2,1)}, u32[]{:S(2)}) copy-start(bf16[12,512,512]{2,1,0:T(8,128)(2,1)} %all-gather.2.cloned.1.call-done) | copy-start | bytes 18874372
  105.7 0.8 copy-start.2
  105.7 0.8 copy-start.3
Sparse Core Ops, SparseCore 0:
  51.6 49.7 all-gather.1
where the time goes:
time: 331 us
  blocking collectives  206 us (62%)
  waiting for transfers between devices  74.3 us (22%)
  starting transfers between devices  13.9 us (4%)
  between operations  13.6 us (4%)
  matrix products  11 us (3%)
  local copies, waits for them, and re-layouts  8.33 us (3%)
  other arithmetic  4.43 us (1%)
    all_to_all x1, blocking collectives, shards(): lax.all_to_all(partial_pairs, 'batch', split_axis=0, concat_axis=0, tiled...  145 us
    all_to_all x1, blocking collectives, shards(): lax.all_to_all(outgoing_sums, 'region', split_axis=0, concat_axis=0, tile...  60.3 us
    all_gather x1, waiting for transfers between devices, shards(): piece = lax.all_gather(fetched, 'batch', axis=1, tiled=True)  49.9 us
    all_to_all x1, waiting for transfers between devices, shards(): lax.all_to_all(outgoing, 'region', split_axis=0, concat_axis=0, tiled=True)  24.3 us
    all_to_all x1, starting transfers between devices, shards(): lax.all_to_all(outgoing, 'region', split_axis=0, concat_axis=0, tiled=True)  13.8 us
  transfers between devices with their start and end apart: 2, of which 2 were waited for; matrix products, arithmetic and copies ran while one was open for 0% of the time, Pallas kernels for 0%

commit v1 on v0

--- a/solution.py
+++ b/solution.py
@@ -48,7 +48,22 @@
     incoming = lax.all_to_all(outgoing, "region", split_axis=0, concat_axis=0, tiled=True)
     flat = incoming.reshape(owner_count * slot_total, row_count, block_width)
     fetched = jnp.take(flat, my_owners * slot_total + my_ranks, axis=0)
-    piece = lax.all_gather(fetched, "batch", axis=1, tiled=True)
+
+    def prepare_steps_all(block_here, across):
+        world = lax.axis_size(across)
+        ledger = list(map(lambda h: (h, (h + 1) % world), range(world)))
+
+        def detail_streams(odd):
+            if len(odd) == world:
+                return odd
+            work_now = detail_streams([lax.ppermute(odd[0], across, ledger), *odd])
+            return work_now
+
+        big = jnp.concatenate(detail_streams([block_here]), axis=1)
+        y1 = jnp.roll(big, (lax.axis_index(across) + 1) * block_here.shape[1], axis=1)
+        return y1
+
+    piece = prepare_steps_all(fetched, "batch")
     count = piece.shape[1]
     shaped = piece.reshape(region_local, 3, count, block_width)
     left_aa = jnp.einsum(

time: 331 us -> 434 us (1.31)
  waiting for transfers between devices: 74.3 us -> 129 us
  local copies, waits for them, and re-layouts: 8.33 us -> 46.8 us
  starting transfers between devices: 13.9 us -> 33.2 us
  between operations: 13.6 us -> 0.28 us
    ppermute x0 -> x15, waiting for transfers between devices: none -> 105 us  [detail_streams(): work_now = detail_streams([lax.ppermute(odd[0], across, ledger), *odd])]
    all_gather x1 -> x0, waiting for transfers between devices: 49.9 us -> none  [shards(): piece = lax.all_gather(fetched, 'batch', axis=1, tiled=True)]
    unnamed x11 -> x61, local copies, waits for them, and re-layouts: 1.72 us -> 37.4 us
    ppermute x0 -> x15, starting transfers between devices: none -> 19.5 us  [detail_streams(): work_now = detail_streams([lax.ppermute(odd[0], across, ledger), *odd])]
    all_to_all x1, blocking collectives: 145 us -> 155 us  [shards(): lax.all_to_all(partial_pairs, 'batch', split_axis=0, concat_axis=0, tiled...]
    all_to_all x1, blocking collectives: 60.3 us -> 55.1 us  [shards(): lax.all_to_all(outgoing_sums, 'region', split_axis=0, concat_axis=0, tile...]
  transfers between devices with their start and end apart: 2 -> 16, of which waited for: 2 -> 16; matrix products, arithmetic and copies ran while one was open for 0% -> 0% of each run, Pallas kernels for 0% -> 0%
where the time goes in v1:
time: 434 us
  blocking collectives  210 us (48%)
  waiting for transfers between devices  129 us (30%)
  local copies, waits for them, and re-layouts  46.8 us (11%)
  starting transfers between devices  33.2 us (8%)
  matrix products  9.31 us (2%)
  other arithmetic  4.45 us (1%)
    all_to_all x1, blocking collectives, shards(): lax.all_to_all(partial_pairs, 'batch', split_axis=0, concat_axis=0, tiled...  155 us
    ppermute x15, waiting for transfers between devices, detail_streams(): work_now = detail_streams([lax.ppermute(odd[0], across, ledger), *odd])  105 us
    all_to_all x1, blocking collectives, shards(): lax.all_to_all(outgoing_sums, 'region', split_axis=0, concat_axis=0, tile...  55.1 us
    unnamed x61, local copies, waits for them, and re-layouts  37.4 us
    all_to_all x1, waiting for transfers between devices, shards(): lax.all_to_all(outgoing, 'region', split_axis=0, concat_axis=0, tiled=True)  24.4 us
    ppermute x15, starting transfers between devices, detail_streams(): work_now = detail_streams([lax.ppermute(odd[0], across, ledger), *odd])  19.5 us
    all_to_all x1, starting transfers between devices, shards(): lax.all_to_all(outgoing, 'region', split_axis=0, concat_axis=0, tiled=True)  13.7 us
  transfers between devices with their start and end apart: 16, of which 16 were waited for; matrix products, arithmetic and copies ran while one was open for 0% of the time, Pallas kernels for 0%

profile of v1, /device:TPU:1, one launch (start us, length us, event | category | flops | bytes accessed | tf_op | source)
XLA Modules:
  0.0 433.6 jit_solution(10479765883469565073)
XLA Ops:
  3.2 13.7 %all-to-all-start = ((bf16[32,1,32,512]{3,2,1,0:T(8,128)(2,1)}), bf16[32,1,32,512]{3,2,1,0:T(8,128)(2,1)S(1)}, u32[]{:S(2)}, u32[]{:S(2)}) async-start(bf16[32,1,32,512]{3,2,1,0:T(8,128)(2,1)} %copy.85), calls=%async_computation | async-start | bytes 2097152 | tf_op jit(solution)/shard_map/all_to_all | solution.py:48
  17.2 24.4 %all-to-all-done = bf16[32,1,32,512]{3,2,1,0:T(8,128)(2,1)S(1)} async-done(((bf16[32,1,32,512]{3,2,1,0:T(8,128)(2,1)}), bf16[32,1,32,512]{3,2,1,0:T(8,128)(2,1)S(1)}, u32[]{:S(2)}, u32[]{:S(2)}) %all-to-all-start) | async-done | bytes 1048608 | tf_op jit(solution)/shard_map/all_to_all | solution.py:48
  42.3 6.2 %collective-permute-start = (bf16[12,32,512]{2,1,0:T(8,128)(2,1)S(1)}, bf16[12,32,512]{2,1,0:T(8,128)(2,1)S(1)}, u32[]{:S(2)}, u32[]{:S(2)}) collective-permute-start(bf16[12,32,512]{2,1,0:T(8,128)(2,1)S(1)} %broadcast_select_fusion), channel_id=1, source_target_pairs={{0,1},{1,2},{2,3},{3,4},{4,5},{5,6},{6,7},{7,8},{8,9},{9,10},{10,1... | collective-permute-start | bytes 1179656 | tf_op jit(solution)/shard_map/ppermute | solution.py:59
  48.4 4.7 %collective-permute-done = bf16[12,32,512]{2,1,0:T(8,128)(2,1)S(1)} collective-permute-done((bf16[12,32,512]{2,1,0:T(8,128)(2,1)S(1)}, bf16[12,32,512]{2,1,0:T(8,128)(2,1)S(1)}, u32[]{:S(2)}, u32[]{:S(2)}) %collective-permute-start) | collective-permute-done | bytes 393248 | tf_op jit(solution)/shard_map/ppermute | solution.py:59
  53.2 2.5 collective-permute-start.1
  55.6 4.7 %collective-permute-done.1 = bf16[12,32,512]{2,1,0:T(8,128)(2,1)S(1)} collective-permute-done((bf16[12,32,512]{2,1,0:T(8,128)(2,1)S(1)}, bf16[12,32,512]{2,1,0:T(8,128)(2,1)S(1)}, u32[]{:S(2)}, u32[]{:S(2)}) %collective-permute-start.1) | collective-permute-done | bytes 393248 | tf_op jit(solution)/shard_map/ppermute | solution.py:59
  60.4 2.5 collective-permute-start.2
  62.8 4.7 %collective-permute-done.2 = bf16[12,32,512]{2,1,0:T(8,128)(2,1)S(1)} collective-permute-done((bf16[12,32,512]{2,1,0:T(8,128)(2,1)S(1)}, bf16[12,32,512]{2,1,0:T(8,128)(2,1)S(1)}, u32[]{:S(2)}, u32[]{:S(2)}) %collective-permute-start.2) | collective-permute-done | bytes 393248 | tf_op jit(solution)/shard_map/ppermute | solution.py:59
  67.6 2.5 collective-permute-start.3
  70.0 4.7 %collective-permute-done.3 = bf16[12,32,512]{2,1,0:T(8,128)(2,1)S(1)} collective-permute-done((bf16[12,32,512]{2,1,0:T(8,128)(2,1)S(1)}, bf16[12,32,512]{2,1,0:T(8,128)(2,1)S(1)}, u32[]{:S(2)}, u32[]{:S(2)}) %collective-permute-start.3) | collective-permute-done | bytes 393248 | tf_op jit(solution)/shard_map/ppermute | solution.py:59
  77.2 4.9 %collective-permute-done.4 = bf16[12,32,512]{2,1,0:T(8,128)(2,1)S(1)} collective-permute-done((bf16[12,32,512]{2,1,0:T(8,128)(2,1)S(1)}, bf16[12,32,512]{2,1,0:T(8,128)(2,1)S(1)}, u32[]{:S(2)}, u32[]{:S(2)}) %collective-permute-start.4) | collective-permute-done | bytes 393248 | tf_op jit(solution)/shard_map/ppermute | solution.py:59
  84.4 6.1 %collective-permute-done.5 = bf16[12,32,512]{2,1,0:T(8,128)(2,1)S(1)} collective-permute-done((bf16[12,32,512]{2,1,0:T(8,128)(2,1)S(1)}, bf16[12,32,512]{2,1,0:T(8,128)(2,1)S(1)}, u32[]{:S(2)}, u32[]{:S(2)}) %collective-permute-start.5) | collective-permute-done | bytes 393248 | tf_op jit(solution)/shard_map/ppermute | solution.py:59
  91.7 7.3 %collective-permute-done.6 = bf16[12,32,512]{2,1,0:T(8,128)(2,1)S(1)} collective-permute-done((bf16[12,32,512]{2,1,0:T(8,128)(2,1)S(1)}, bf16[12,32,512]{2,1,0:T(8,128)(2,1)S(1)}, u32[]{:S(2)}, u32[]{:S(2)}) %collective-permute-start.6) | collective-permute-done | bytes 393248 | tf_op jit(solution)/shard_map/ppermute | solution.py:59
  99.0 8.4 %collective-permute-done.7 = bf16[12,32,512]{2,1,0:T(8,128)(2,1)S(1)} collective-permute-done((bf16[12,32,512]{2,1,0:T(8,128)(2,1)S(1)}, bf16[12,32,512]{2,1,0:T(8,128)(2,1)S(1)}, u32[]{:S(2)}, u32[]{:S(2)}) %collective-permute-start.7) | collective-permute-done | bytes 393248 | tf_op jit(solution)/shard_map/ppermute | solution.py:59
  107.4 8.4 %collective-permute-done.8 = bf16[12,32,512]{2,1,0:T(8,128)(2,1)S(1)} collective-permute-done((bf16[12,32,512]{2,1,0:T(8,128)(2,1)S(1)}, bf16[12,32,512]{2,1,0:T(8,128)(2,1)S(1)}, u32[]{:S(2)}, u32[]{:S(2)}) %collective-permute-start.8) | collective-permute-done | bytes 393248 | tf_op jit(solution)/shard_map/ppermute | solution.py:59
  116.6 8.4 %collective-permute-done.9 = bf16[12,32,512]{2,1,0:T(8,128)(2,1)S(1)} collective-permute-done((bf16[12,32,512]{2,1,0:T(8,128)(2,1)S(1)}, bf16[12,32,512]{2,1,0:T(8,128)(2,1)S(1)}, u32[]{:S(2)}, u32[]{:S(2)}) %collective-permute-start.9) | collective-permute-done | bytes 393248 | tf_op jit(solution)/shard_map/ppermute | solution.py:59
  125.7 8.4 %collective-permute-done.10 = bf16[12,32,512]{2,1,0:T(8,128)(2,1)S(1)} collective-permute-done((bf16[12,32,512]{2,1,0:T(8,128)(2,1)S(1)}, bf16[12,32,512]{2,1,0:T(8,128)(2,1)S(1)}, u32[]{:S(2)}, u32[]{:S(2)}) %collective-permute-start.10) | collective-permute-done | bytes 393248 | tf_op jit(solution)/shard_map/ppermute | solution.py:59
  134.9 8.4 %collective-permute-done.11 = bf16[12,32,512]{2,1,0:T(8,128)(2,1)S(1)} collective-permute-done((bf16[12,32,512]{2,1,0:T(8,128)(2,1)S(1)}, bf16[12,32,512]{2,1,0:T(8,128)(2,1)S(1)}, u32[]{:S(2)}, u32[]{:S(2)}) %collective-permute-start.11) | collective-permute-done | bytes 393248 | tf_op jit(solution)/shard_map/ppermute | solution.py:59
  144.1 8.4 %collective-permute-done.12 = bf16[12,32,512]{2,1,0:T(8,128)(2,1)S(1)} collective-permute-done((bf16[12,32,512]{2,1,0:T(8,128)(2,1)S(1)}, bf16[12,32,512]{2,1,0:T(8,128)(2,1)S(1)}, u32[]{:S(2)}, u32[]{:S(2)}) %collective-permute-start.12) | collective-permute-done | bytes 393248 | tf_op jit(solution)/shard_map/ppermute | solution.py:59
  153.2 8.5 %collective-permute-done.13 = bf16[12,32,512]{2,1,0:T(8,128)(2,1)} collective-permute-done((bf16[12,32,512]{2,1,0:T(8,128)(2,1)S(1)}, bf16[12,32,512]{2,1,0:T(8,128)(2,1)}, u32[]{:S(2)}, u32[]{:S(2)}) %collective-permute-start.13) | collective-permute-done | bytes 393248 | tf_op jit(solution)/shard_map/ppermute | solution.py:59
  161.8 8.7 %collective-permute-done.14 = bf16[12,32,512]{2,1,0:T(8,128)(2,1)} collective-permute-done((bf16[12,32,512]{2,1,0:T(8,128)(2,1)}, bf16[12,32,512]{2,1,0:T(8,128)(2,1)}, u32[]{:S(2)}, u32[]{:S(2)}) %collective-permute-start.14) | collective-permute-done | bytes 393248 | tf_op jit(solution)/shard_map/ppermute | solution.py:59
  205.1 3.6 constant_dynamic-slice_fusion
  216.4 155.1 %all_to_all.15 = bf16[16,32,12,512]{3,1,2,0:T(8,128)(2,1)S(1)} all-to-all(bf16[16,32,12,512]{3,1,2,0:T(8,128)(2,1)S(1)} %copy.97), channel_id=1, replica_groups=mesh['region'=32,'batch'=16] {'batch'}, dimensions={0} | all-to-all | bytes 12582912 | tf_op jit(solution)/shard_map/all_to_all | solution.py:99
  375.4 55.1 %all_to_all.16 = f32[32,1,32,512]{3,2,1,0:T(8,128)S(1)} all-to-all(f32[32,1,32,512]{3,2,1,0:T(8,128)S(1)} %copy.100), channel_id=1, replica_groups=mesh['region'=32,'batch'=16] {'region'}, dimensions={0} | all-to-all | bytes 4194304 | tf_op jit(solution)/shard_map/all_to_all | solution.py:106
  (104 shorter events, 62.9 us)
Async XLA Ops:
  3.2 38.3 %all-to-all-start = ((bf16[32,1,32,512]{3,2,1,0:T(8,128)(2,1)}), bf16[32,1,32,512]{3,2,1,0:T(8,128)(2,1)S(1)}, u32[]{:S(2)}, u32[]{:S(2)}) async-start(bf16[32,1,32,512]{3,2,1,0:T(8,128)(2,1)} %copy.85), calls=%async_computation | async-start | bytes 2097152 | tf_op jit(solution)/shard_map/all_to_all | solution.py:48
  42.3 10.9 %collective-permute-start = (bf16[12,32,512]{2,1,0:T(8,128)(2,1)S(1)}, bf16[12,32,512]{2,1,0:T(8,128)(2,1)S(1)}, u32[]{:S(2)}, u32[]{:S(2)}) collective-permute-start(bf16[12,32,512]{2,1,0:T(8,128)(2,1)S(1)} %broadcast_select_fusion), channel_id=1, source_target_pairs={{0,1},{1,2},{2,3},{3,4},{4,5},{5,6},{6,7},{7,8},{8,9},{9,10},{10,1... | collective-permute-start | bytes 1179656 | tf_op jit(solution)/shard_map/ppermute | solution.py:59
  53.2 7.2 %collective-permute-start.1 = (bf16[12,32,512]{2,1,0:T(8,128)(2,1)S(1)}, bf16[12,32,512]{2,1,0:T(8,128)(2,1)S(1)}, u32[]{:S(2)}, u32[]{:S(2)}) collective-permute-start(bf16[12,32,512]{2,1,0:T(8,128)(2,1)S(1)} %collective-permute-done), channel_id=1, source_target_pairs={{0,1},{1,2},{2,3},{3,4},{4,5},{5,6},{6,7},{7,8},{8,9},{9,10},{10,1... | collective-permute-start | bytes 1179656 | tf_op jit(solution)/shard_map/ppermute | solution.py:59
  60.4 7.2 %collective-permute-start.2 = (bf16[12,32,512]{2,1,0:T(8,128)(2,1)S(1)}, bf16[12,32,512]{2,1,0:T(8,128)(2,1)S(1)}, u32[]{:S(2)}, u32[]{:S(2)}) collective-permute-start(bf16[12,32,512]{2,1,0:T(8,128)(2,1)S(1)} %collective-permute-done.1), channel_id=1, source_target_pairs={{0,1},{1,2},{2,3},{3,4},{4,5},{5,6},{6,7},{7,8},{8,9},{9,10},{10,1... | collective-permute-start | bytes 1179656 | tf_op jit(solution)/shard_map/ppermute | solution.py:59
  67.6 7.2 %collective-permute-start.3 = (bf16[12,32,512]{2,1,0:T(8,128)(2,1)S(1)}, bf16[12,32,512]{2,1,0:T(8,128)(2,1)S(1)}, u32[]{:S(2)}, u32[]{:S(2)}) collective-permute-start(bf16[12,32,512]{2,1,0:T(8,128)(2,1)S(1)} %collective-permute-done.2), channel_id=1, source_target_pairs={{0,1},{1,2},{2,3},{3,4},{4,5},{5,6},{6,7},{7,8},{8,9},{9,10},{10,1... | collective-permute-start | bytes 1179656 | tf_op jit(solution)/shard_map/ppermute | solution.py:59
  74.8 7.4 %collective-permute-start.4 = (bf16[12,32,512]{2,1,0:T(8,128)(2,1)S(1)}, bf16[12,32,512]{2,1,0:T(8,128)(2,1)S(1)}, u32[]{:S(2)}, u32[]{:S(2)}) collective-permute-start(bf16[12,32,512]{2,1,0:T(8,128)(2,1)S(1)} %collective-permute-done.3), channel_id=1, source_target_pairs={{0,1},{1,2},{2,3},{3,4},{4,5},{5,6},{6,7},{7,8},{8,9},{9,10},{10,1... | collective-permute-start | bytes 1179656 | tf_op jit(solution)/shard_map/ppermute | solution.py:59
  82.1 8.4 %collective-permute-start.5 = (bf16[12,32,512]{2,1,0:T(8,128)(2,1)S(1)}, bf16[12,32,512]{2,1,0:T(8,128)(2,1)S(1)}, u32[]{:S(2)}, u32[]{:S(2)}) collective-permute-start(bf16[12,32,512]{2,1,0:T(8,128)(2,1)S(1)} %collective-permute-done.4), channel_id=1, source_target_pairs={{0,1},{1,2},{2,3},{3,4},{4,5},{5,6},{6,7},{7,8},{8,9},{9,10},{10,1... | collective-permute-start | bytes 1179656 | tf_op jit(solution)/shard_map/ppermute | solution.py:59
  90.5 8.4 %collective-permute-start.6 = (bf16[12,32,512]{2,1,0:T(8,128)(2,1)S(1)}, bf16[12,32,512]{2,1,0:T(8,128)(2,1)S(1)}, u32[]{:S(2)}, u32[]{:S(2)}) collective-permute-start(bf16[12,32,512]{2,1,0:T(8,128)(2,1)S(1)} %collective-permute-done.5), channel_id=1, source_target_pairs={{0,1},{1,2},{2,3},{3,4},{4,5},{5,6},{6,7},{7,8},{8,9},{9,10},{10,1... | collective-permute-start | bytes 1179656 | tf_op jit(solution)/shard_map/ppermute | solution.py:59
  99.0 8.4 %collective-permute-start.7 = (bf16[12,32,512]{2,1,0:T(8,128)(2,1)S(1)}, bf16[12,32,512]{2,1,0:T(8,128)(2,1)S(1)}, u32[]{:S(2)}, u32[]{:S(2)}) collective-permute-start(bf16[12,32,512]{2,1,0:T(8,128)(2,1)S(1)} %collective-permute-done.6), channel_id=1, source_target_pairs={{0,1},{1,2},{2,3},{3,4},{4,5},{5,6},{6,7},{7,8},{8,9},{9,10},{10,1... | collective-permute-start | bytes 1179656 | tf_op jit(solution)/shard_map/ppermute | solution.py:59
  107.4 8.4 %collective-permute-start.8 = (bf16[12,32,512]{2,1,0:T(8,128)(2,1)S(1)}, bf16[12,32,512]{2,1,0:T(8,128)(2,1)S(1)}, u32[]{:S(2)}, u32[]{:S(2)}) collective-permute-start(bf16[12,32,512]{2,1,0:T(8,128)(2,1)S(1)} %collective-permute-done.7), channel_id=1, source_target_pairs={{0,1},{1,2},{2,3},{3,4},{4,5},{5,6},{6,7},{7,8},{8,9},{9,10},{10,1... | collective-permute-start | bytes 1179656 | tf_op jit(solution)/shard_map/ppermute | solution.py:59
  116.6 8.4 %collective-permute-start.9 = (bf16[12,32,512]{2,1,0:T(8,128)(2,1)S(1)}, bf16[12,32,512]{2,1,0:T(8,128)(2,1)S(1)}, u32[]{:S(2)}, u32[]{:S(2)}) collective-permute-start(bf16[12,32,512]{2,1,0:T(8,128)(2,1)S(1)} %collective-permute-done.8), channel_id=1, source_target_pairs={{0,1},{1,2},{2,3},{3,4},{4,5},{5,6},{6,7},{7,8},{8,9},{9,10},{10,1... | collective-permute-start | bytes 1179656 | tf_op jit(solution)/shard_map/ppermute | solution.py:59
  125.7 8.4 %collective-permute-start.10 = (bf16[12,32,512]{2,1,0:T(8,128)(2,1)S(1)}, bf16[12,32,512]{2,1,0:T(8,128)(2,1)S(1)}, u32[]{:S(2)}, u32[]{:S(2)}) collective-permute-start(bf16[12,32,512]{2,1,0:T(8,128)(2,1)S(1)} %collective-permute-done.9), channel_id=1, source_target_pairs={{0,1},{1,2},{2,3},{3,4},{4,5},{5,6},{6,7},{7,8},{8,9},{9,10},{10,1... | collective-permute-start | bytes 1179656 | tf_op jit(solution)/shard_map/ppermute | solution.py:59
  134.9 8.4 %collective-permute-start.11 = (bf16[12,32,512]{2,1,0:T(8,128)(2,1)S(1)}, bf16[12,32,512]{2,1,0:T(8,128)(2,1)S(1)}, u32[]{:S(2)}, u32[]{:S(2)}) collective-permute-start(bf16[12,32,512]{2,1,0:T(8,128)(2,1)S(1)} %collective-permute-done.10), channel_id=1, source_target_pairs={{0,1},{1,2},{2,3},{3,4},{4,5},{5,6},{6,7},{7,8},{8,9},{9,10},{10,1... | collective-permute-start | bytes 1179656 | tf_op jit(solution)/shard_map/ppermute | solution.py:59
  144.1 8.4 %collective-permute-start.12 = (bf16[12,32,512]{2,1,0:T(8,128)(2,1)S(1)}, bf16[12,32,512]{2,1,0:T(8,128)(2,1)S(1)}, u32[]{:S(2)}, u32[]{:S(2)}) collective-permute-start(bf16[12,32,512]{2,1,0:T(8,128)(2,1)S(1)} %collective-permute-done.11), channel_id=1, source_target_pairs={{0,1},{1,2},{2,3},{3,4},{4,5},{5,6},{6,7},{7,8},{8,9},{9,10},{10,1... | collective-permute-start | bytes 1179656 | tf_op jit(solution)/shard_map/ppermute | solution.py:59
  153.2 8.5 %collective-permute-start.13 = (bf16[12,32,512]{2,1,0:T(8,128)(2,1)S(1)}, bf16[12,32,512]{2,1,0:T(8,128)(2,1)}, u32[]{:S(2)}, u32[]{:S(2)}) collective-permute-start(bf16[12,32,512]{2,1,0:T(8,128)(2,1)S(1)} %collective-permute-done.12), channel_id=1, source_target_pairs={{0,1},{1,2},{2,3},{3,4},{4,5},{5,6},{6,7},{7,8},{8,9},{9,10},{10,1... | collective-permute-start | bytes 1179656 | tf_op jit(solution)/shard_map/ppermute | solution.py:59
  161.8 8.7 %collective-permute-start.14 = (bf16[12,32,512]{2,1,0:T(8,128)(2,1)}, bf16[12,32,512]{2,1,0:T(8,128)(2,1)}, u32[]{:S(2)}, u32[]{:S(2)}) collective-permute-start(bf16[12,32,512]{2,1,0:T(8,128)(2,1)} %collective-permute-done.13), channel_id=1, source_target_pairs={{0,1},{1,2},{2,3},{3,4},{4,5},{5,6},{6,7},{7,8},{8,9},{9,10},{10,1... | collective-permute-start | bytes 1179656 | tf_op jit(solution)/shard_map/ppermute | solution.py:59
  161.8 32.1 %copy-start.12 = (bf16[12,32,512]{2,1,0:T(8,128)(2,1)S(1)}, bf16[12,32,512]{2,1,0:T(8,128)(2,1)}, u32[]{:S(2)}) copy-start(bf16[12,32,512]{2,1,0:T(8,128)(2,1)} %copy-done.11) | copy-start | bytes 1179652
  161.8 32.9 %copy-start.10 = (bf16[12,32,512]{2,1,0:T(8,128)(2,1)S(1)}, bf16[12,32,512]{2,1,0:T(8,128)(2,1)}, u32[]{:S(2)}) copy-start(bf16[12,32,512]{2,1,0:T(8,128)(2,1)} %copy-done.9) | copy-start | bytes 1179652
  161.8 33.7 %copy-start.8 = (bf16[12,32,512]{2,1,0:T(8,128)(2,1)S(1)}, bf16[12,32,512]{2,1,0:T(8,128)(2,1)}, u32[]{:S(2)}) copy-start(bf16[12,32,512]{2,1,0:T(8,128)(2,1)} %copy-done.7) | copy-start | bytes 1179652
  161.8 34.5 %copy-start.6 = (bf16[12,32,512]{2,1,0:T(8,128)(2,1)S(1)}, bf16[12,32,512]{2,1,0:T(8,128)(2,1)}, u32[]{:S(2)}) copy-start(bf16[12,32,512]{2,1,0:T(8,128)(2,1)} %copy-done.5) | copy-start | bytes 1179652
  161.8 35.3 %copy-start.4 = (bf16[12,32,512]{2,1,0:T(8,128)(2,1)S(1)}, bf16[12,32,512]{2,1,0:T(8,128)(2,1)}, u32[]{:S(2)}) copy-start(bf16[12,32,512]{2,1,0:T(8,128)(2,1)} %copy-done.3) | copy-start | bytes 1179652
  190.2 18.5 %copy-start.2 = (bf16[4,2,256,512]{3,2,1,0:T(8,128)(2,1)S(1)}, bf16[4,2,256,512]{3,2,1,0:T(8,128)(2,1)}, u32[]{:S(2)}) copy-start(bf16[4,2,256,512]{3,2,1,0:T(8,128)(2,1)} %param.5) | copy-start | bytes 6291460
  208.6 2.4 copy-start.13
  216.4 217.2 %copy-start.1 = (bf16[4,32,512]{2,1,0:T(8,128)(2,1)S(1)}, bf16[4,32,512]{2,1,0:T(8,128)(2,1)}, u32[]{:S(2)}) copy-start(bf16[4,32,512]{2,1,0:T(8,128)(2,1)} %param.6) | copy-start | bytes 393220
  (7 other events, 7.4 us)
